TPU v7x, 32 devices: a whole 2x2x4 slice. The times are simulated.
32 devices in a mesh: view: 8 (over z, core), span: 4 (over y, x).
Axes of the slice: x: 2, y: 2, z: 4, core: 2. Of those that a mesh axis runs over, the one named last changes fastest.
Arguments:
- tokens: bfloat16 [8, 1024, 1024], P('view', 'span'), may hold values from -6 to 6
- scan_order: int32 [8, 1024], P('view'), may hold values from 0 to 1023, as said below
- w_merge: bfloat16 [4096, 1024], replicated, may hold values from -0.09375 to 0.09375
- bias: bfloat16 [1024], replicated, may hold values from -4 to 4
- cotangent: bfloat16 [8, 256, 1024], P('view', 'span'), may hold values from -6 to 6
Outputs:
- merged_out: bfloat16 [8, 256, 1024], P('view', 'span')
- token_grad: bfloat16 [8, 1024, 1024], P('view', 'span')
- weight_grad: float32 [4096, 1024], P(('view', 'span'))
- bias_grad: float32 [1024], replicated
Inputs may be any that keep to these rules, and one draw needn't show every extreme that they name: `scan_order`: each row is a permutation of the raster indices of one view. Call tokens 256 * b to 256 * (b + 1) - 1 band b, and scan positions 256 * c to 256 * (c + 1) - 1 block c: every block holds at most 96 tokens of any band, and in every row each block holds exactly 96 tokens of some band.
All inputs are finite; a program needn't handle non-finite values.
Results may differ from a plain program's by a relative error of at most 0.001.
Values may be sent and summed in bfloat16 or wider, within the bound.
No kernel may reach another device: no remote copies, remote signals or barrier semaphores. Data moves between devices by JAX's collectives and lax.ppermute only.
A program may use at most 128 MiB of HBM per device.

v0:
```python
import math
import jax
import jax.numpy as jnp
from jax import lax
from jax.sharding import PartitionSpec as P

COLS = 128


def body(tokens, scan_order, w_merge, bias, cotangent):
    spans = lax.axis_size("span")
    views = lax.axis_size("view")
    span_index = lax.axis_index("span")
    tok_dev = tokens.shape[1]
    width = tokens.shape[2]
    capacity = 3 * (tok_dev // spans) // 2
    rows_dev = tok_dev // COLS
    order_all = scan_order[0].reshape(spans, tok_dev)
    owners = order_all // tok_dev
    owner_hot = (owners[:, :, None] == jnp.arange(spans, dtype=jnp.int32)[None, None, :]).astype(
        jnp.int32
    )
    slot_rank = jnp.sum((jnp.cumsum(owner_hot, axis=1) - 1) * owner_hot, axis=2)
    dest_slots = owners * capacity + slot_rank
    my_slots = lax.dynamic_index_in_dim(dest_slots, span_index, 0, keepdims=False)
    outgoing = jnp.zeros((spans * capacity, width), jnp.bfloat16).at[my_slots].set(tokens[0])
    received = lax.all_to_all(
        outgoing.reshape(spans, capacity, width), "span", split_axis=0, concat_axis=0, tiled=True
    )
    arriving = owners == span_index
    source_slot = jnp.arange(spans, dtype=jnp.int32)[:, None] * capacity + slot_rank
    local_index = jnp.where(arriving, order_all - span_index * tok_dev, tok_dev)
    source_of = (
        jnp.zeros((tok_dev,), jnp.int32)
        .at[local_index.reshape(-1)]
        .set(source_slot.reshape(-1), mode="drop")
    )
    raster = received.reshape(spans * capacity, width)[source_of]
    merged = (
        raster.reshape(rows_dev // 2, 2, COLS // 2, 2, width)
        .transpose(0, 2, 1, 3, 4)
        .reshape(tok_dev // 4, 4 * width)
    )
    merged_out = (
        jnp.dot(merged, w_merge, preferred_element_type=jnp.float32) + bias.astype(jnp.float32)
    ).astype(jnp.bfloat16)
    grads = cotangent[0]
    grad_merged = lax.dot_general(
        grads, w_merge, (((1,), (1,)), ((), ())), preferred_element_type=jnp.float32
    ).astype(jnp.bfloat16)
    grad_raster = (
        grad_merged.reshape(rows_dev // 2, COLS // 2, 2, 2, width)
        .transpose(0, 2, 1, 3, 4)
        .reshape(tok_dev, width)
    )
    going_back = jnp.zeros((spans * capacity, width), jnp.bfloat16).at[source_of].set(grad_raster)
    returned = lax.all_to_all(
        going_back.reshape(spans, capacity, width), "span", split_axis=0, concat_axis=0, tiled=True
    )
    token_grad = returned.reshape(spans * capacity, width)[my_slots]
    kernel_rows = 4 * width
    merged_rows = merged.shape[0]
    group_rows = kernel_rows // (views * spans)
    regrouped = merged.reshape(merged_rows, views, spans, group_rows).transpose(0, 2, 1, 3)
    view_tokens = lax.all_to_all(regrouped, "span", split_axis=1, concat_axis=0, tiled=True)
    view_tokens = view_tokens.reshape(spans * merged_rows, views * group_rows)
    all_grads = lax.all_gather(grads, "span", axis=0, tiled=True)
    partial_sum = lax.dot_general(
        view_tokens, all_grads, (((0,), (0,)), ((), ())), preferred_element_type=jnp.float32
    )
    weight_sum = lax.psum_scatter(partial_sum, "view", scatter_dimension=0, tiled=True)
    bias_total = lax.psum(jnp.sum(grads.astype(jnp.float32), axis=0), ("view", "span"))
    grad_scale = 1.0 / math.sqrt(views * spans * (tok_dev // 4))
    return (merged_out[None], token_grad[None], weight_sum * grad_scale, bias_total * grad_scale)


def solution(mesh):
    in_specs = (P("view", "span", None), P("view", None), P(), P(), P("view", "span", None))
    out_specs = (P("view", "span", None), P("view", "span", None), P(("view", "span"), None), P())
    return jax.shard_map(body, mesh=mesh, in_specs=in_specs, out_specs=out_specs, check_vma=False)
```

profile of v0, /device:TPU:0, one launch (start us, length us, event | category | flops | bytes accessed | tf_op | source)
XLA Modules:
  0.0 131.2 jit_solution(6496516762859729099)
XLA Ops:
  7.2 0.8 and_select_fusion.1
  8.0 4.8 %reduce-window.6 = s32[4,4,2,128]{3,2,1,0:T(2,128)S(1)} reduce-window(s32[4,4,2,128]{3,2,1,0:T(2,128)S(1)} %compare_convert_fusion, s32[]{:T(128)} %constant.19.clone.1), window={size=1x1x1x128 pad=0_0x0_0x0_0x127_0}, to_apply=%region_0.1 | reduce-window | flops 520192 | bytes 32772 | tf_op jit(solution)/shard_map/reduce-window
  13.3 0.5 broadcast.237
  13.8 1.3 %reduce.3 = s32[1024]{0:T(1024)S(1)} reduce(s32[1,1024]{1,0:T(1,128)} %param.6, s32[]{:T(128)} %broadcast.237), dimensions={0}, to_apply=%param.6.reduce_sub_computation.3 | reduce | bytes 8196 | tf_op args[1]
  15.2 2.6 %scatter_custom_fusion = bf16[384,1024]{1,0:T(8,128)(2,1)} fusion(s32[256]{0:T(256)S(1)} %bitcast.75, bf16[1,256,1024]{2,1,0:T(8,128)(2,1)S(1)} %copy-done, bf16[]{:T(256)} %constant.15.clone.1), kind=kCustom, calls=%fused_computation.13 | custom fusion | bytes 1310722 | tf_op jit(solution)/shard_map/scatter | solution.py:26
  17.8 5.2 %all-to-all-start = ((bf16[4,96,1024]{2,1,0:T(8,128)(2,1)}), bf16[4,96,1024]{2,1,0:T(8,128)(2,1)S(1)}, u32[]{:S(2)}, u32[]{:S(2)}) async-start(bf16[4,96,1024]{2,1,0:T(8,128)(2,1)} %bitcast.6), calls=%async_computation | async-start | bytes 1572864 | tf_op jit(solution)/shard_map/all_to_all | solution.py:27
  23.1 0.7 compare_select_fusion
  23.8 4.3 %scatter_custom_fusion.1 = s32[256]{0:T(256)S(1)} fusion(s32[1024]{0:T(1024)S(1)} %bitcast.78, s32[1024]{0:T(1024)S(1)} %bitcast.77, s32[]{:T(128)} %constant.19.clone.1), kind=kCustom, calls=%fused_computation.59 | custom fusion | bytes 1028 | tf_op jit(solution)/shard_map/scatter | solution.py:36
  28.2 5.7 %all-to-all-done = bf16[4,96,1024]{2,1,0:T(8,128)(2,1)S(1)} async-done(((bf16[4,96,1024]{2,1,0:T(8,128)(2,1)}), bf16[4,96,1024]{2,1,0:T(8,128)(2,1)S(1)}, u32[]{:S(2)}, u32[]{:S(2)}) %all-to-all-start) | async-done | bytes 786464 | tf_op jit(solution)/shard_map/all_to_all | solution.py:27
  33.8 1.2 gather_fusion
  35.9 0.9 copy.20
  36.8 3.5 %all-to-all-start.2 = ((bf16[64,4,8,128]{3,2,0,1:T(8,128)(2,1)}), bf16[64,4,8,128]{3,2,0,1:T(8,128)(2,1)S(1)}, u32[]{:S(2)}, u32[]{:S(2)}) async-start(bf16[64,4,8,128]{3,2,0,1:T(8,128)(2,1)} %copy.20), calls=%async_computation.2 | async-start | bytes 1048576 | tf_op jit(solution)/shard_map/all_to_all | solution.py:65
  40.3 13.7 %all-gather = bf16[1,256,1024]{2,1,0:T(8,128)(2,1)S(1)} all-gather(bf16[1,64,1024]{2,1,0:T(8,128)(2,1)S(1)} %copy-done.1), channel_id=2, replica_groups=mesh['view'=8,'span'=4] {'span'}, dimensions={1}, use_global_device_ids=true | all-gather | bytes 655360 | tf_op jit(solution)/shard_map/all_gather | solution.py:67
  54.0 2.7 %fusion.2 = f32[1024,1024]{1,0:T(8,128)} fusion(bf16[32,8,8,128]{3,2,1,0:T(8,128)(2,1)S(1)} %bitcast.70, bf16[1,256,1024]{2,1,0:T(8,128)(2,1)S(1)} %all-gather), kind=kOutput, calls=%fused_computation.9 | convolution fusion | flops 536870912 | bytes 5242880 | tf_op jit(solution)/shard_map/dot_general | solution.py:68
  56.7 6.0 %convolution_convert_fusion = bf16[64,4096]{1,0:T(8,128)(2,1)S(1)} fusion(bf16[4096,1024]{1,0:T(8,128)(2,1)} %param.7, bf16[1,64,1024]{2,1,0:T(8,128)(2,1)S(1)} %copy-done.1), kind=kOutput, calls=%fused_computation.5 | convolution fusion | flops 537133056 | bytes 9043968 | tf_op jit(solution)/shard_map/dot_general | solution.py:48
  62.8 0.4 reshape.226
  63.7 2.6 %scatter_custom_fusion.2 = bf16[384,1024]{1,0:T(8,128)(2,1)} fusion(s32[256]{0:T(256)S(1)} %compare_select_fusion.6, bf16[256,1024]{1,0:T(8,128)(2,1)S(1)} %reshape.267, bf16[]{:T(256)} %constant.15.clone.1), kind=kCustom, calls=%fused_computation.17 | custom fusion | bytes 786434 | tf_op jit(solution)/shard_map/scatter | solution.py:56
  66.3 3.5 %all-to-all-start.1 = ((bf16[4,96,1024]{2,1,0:T(8,128)(2,1)}), bf16[4,96,1024]{2,1,0:T(8,128)(2,1)S(1)}, u32[]{:S(2)}, u32[]{:S(2)}) async-start(bf16[4,96,1024]{2,1,0:T(8,128)(2,1)} %bitcast.14), calls=%async_computation.1 | async-start | bytes 1572864 | tf_op jit(solution)/shard_map/all_to_all | solution.py:57
  69.9 44.0 %psum.7 = f32[1024]{0:T(1024)S(1)} all-reduce(f32[1024]{0:T(1024)S(1)} %convert_reduce_fusion), channel_id=1, replica_groups=mesh['view'=8,'span'=4] {'view','span'}, use_global_device_ids=true, to_apply=%region_8.9 | all-reduce | flops 1024 | bytes 8192 | tf_op jit(solution)/shard_map/psum | solution.py:72
  113.8 0.6 broadcast_multiply_fusion.1
  114.4 0.4 reshape.225
  114.8 2.0 %gather_fusion.1 = bf16[256,1024]{1,0:T(8,128)(2,1)} fusion(bf16[384,1024]{1,0:T(8,128)(2,1)S(1)} %bitcast.67, s32[1024]{0:T(1024)S(1)} %pad_clamp_fusion), kind=kCustom, calls=%fused_computation.1 | custom fusion | bytes 1049600 | tf_op jit(solution)/shard_map/gather | solution.py:60
  116.8 5.6 %fusion.1 = bf16[1,64,1024]{2,1,0:T(8,128)(2,1)} fusion(bf16[64,4096]{1,0:T(8,128)(2,1)S(1)} %reshape.225, bf16[4096,1024]{1,0:T(8,128)(2,1)} %param.7, f32[1024]{0:T(1024)S(1)} %convert_element_type.18), kind=kOutput, calls=%fused_computation.8 | convolution fusion | flops 537001984 | bytes 9048064 | tf_op jit(solution)/shard_map/dot_general | solution.py:45
  122.4 1.9 %broadcast_multiply_fusion = f32[128,1024]{1,0:T(8,128)} fusion(f32[128,1024]{1,0:T(8,128)} %reduce-scatter.2.cloned.1.call-done), kind=kLoop, calls=%fused_computation.21 | loop fusion | flops 131072 | bytes 1048576 | tf_op jit(solution)/shard_map/mul | solution.py:74
  (36 shorter events, 2.2 us)
Async XLA Ops:
  7.2 8.1 %copy-start = (bf16[1,256,1024]{2,1,0:T(8,128)(2,1)S(1)}, bf16[1,256,1024]{2,1,0:T(8,128)(2,1)}, u32[]{:S(2)}) copy-start(bf16[1,256,1024]{2,1,0:T(8,128)(2,1)} %param.5) | copy-start | bytes 1572868
  7.2 33.1 %copy-start.1 = (bf16[1,64,1024]{2,1,0:T(8,128)(2,1)S(1)}, bf16[1,64,1024]{2,1,0:T(8,128)(2,1)}, u32[]{:S(2)}) copy-start(bf16[1,64,1024]{2,1,0:T(8,128)(2,1)} %param.9) | copy-start | bytes 393220
  17.8 16.0 %all-to-all-start = ((bf16[4,96,1024]{2,1,0:T(8,128)(2,1)}), bf16[4,96,1024]{2,1,0:T(8,128)(2,1)S(1)}, u32[]{:S(2)}, u32[]{:S(2)}) async-start(bf16[4,96,1024]{2,1,0:T(8,128)(2,1)} %bitcast.6), calls=%async_computation | async-start | bytes 1572864 | tf_op jit(solution)/shard_map/all_to_all | solution.py:27
  36.8 17.2 %all-to-all-start.2 = ((bf16[64,4,8,128]{3,2,0,1:T(8,128)(2,1)}), bf16[64,4,8,128]{3,2,0,1:T(8,128)(2,1)S(1)}, u32[]{:S(2)}, u32[]{:S(2)}) async-start(bf16[64,4,8,128]{3,2,0,1:T(8,128)(2,1)} %copy.20), calls=%async_computation.2 | async-start | bytes 1048576 | tf_op jit(solution)/shard_map/all_to_all | solution.py:65
  40.3 82.2 %reduce-scatter.2.cloned.1.call-start = ((), (), s32[]{:S(2)}) async-start(), calls=%async_computation.4 | async-start | bytes 4718592 | tf_op jit(solution)/shard_map/reduce_scatter | solution.py:71
  56.7 13.1 %copy-start.2 = (bf16[1024]{0:T(1024)(128)(2,1)S(1)}, bf16[1024]{0:T(1024)(128)(2,1)}, u32[]{:S(2)}) copy-start(bf16[1024]{0:T(1024)(128)(2,1)} %param.8) | copy-start | bytes 6148
  66.3 48.5 %all-to-all-start.1 = ((bf16[4,96,1024]{2,1,0:T(8,128)(2,1)}), bf16[4,96,1024]{2,1,0:T(8,128)(2,1)S(1)}, u32[]{:S(2)}, u32[]{:S(2)}) async-start(bf16[4,96,1024]{2,1,0:T(8,128)(2,1)} %bitcast.14), calls=%async_computation.1 | async-start | bytes 1572864 | tf_op jit(solution)/shard_map/all_to_all | solution.py:57
Sparse Core Ops, SparseCore 0:
  56.8 51.2 reduce-scatter.1
where the time goes:
time: 132 us; the launch traced here: 131 us
  blocking collectives  57.6 us (44%)
  local copies, waits for them, and re-layouts  16.6 us (13%)
  matrix products  14.3 us (11%)
  between operations  14.2 us (11%)
  starting transfers between devices  12.2 us (9%)
  other arithmetic  10.4 us (8%)
  waiting for transfers between devices  5.71 us (4%)
    psum x1, blocking collectives, body(): lax.psum(jnp.sum(grads.astype(jnp.float32), axis=0), ('view', 'span'))  44 us
    all_gather x1, blocking collectives, body(): all_grads = lax.all_gather(grads, 'span', axis=0, tiled=True)  13.7 us
    dot_general x1, matrix products, body(): lax.dot_general(grads, w_merge, (((1,), (1,)), ((), ())), preferred_eleme...  6.04 us
    all_to_all x1, waiting for transfers between devices, body(): lax.all_to_all(outgoing.reshape(spans, capacity, width), 'span', split_ax...  5.69 us
    dot_general x1, matrix products, body(): jnp.dot(merged, w_merge, preferred_element_type=jnp.float32)  5.61 us
    all_to_all x1, starting transfers between devices, body(): lax.all_to_all(outgoing.reshape(spans, capacity, width), 'span', split_ax...  5.19 us
    another operation x2, other arithmetic  4.84 us
    scatter x1, local copies, waits for them, and re-layouts, body(): source_of = jnp.zeros((tok_dev,), jnp.int32).at[local_index.reshape(-1)]....  4.3 us
  transfers between devices with their start and end apart: 4, of which 1 were waited for; matrix products, arithmetic and copies ran while one was open for 18% of the time, Pallas kernels for 0%

commit v1 on v0

--- a/solution.py
+++ b/solution.py
@@ -69,7 +69,9 @@
         view_tokens, all_grads, (((0,), (0,)), ((), ())), preferred_element_type=jnp.float32
     )
     weight_sum = lax.psum_scatter(partial_sum, "view", scatter_dimension=0, tiled=True)
-    bias_total = lax.psum(jnp.sum(grads.astype(jnp.float32), axis=0), ("view", "span"))
+    bias_total = jnp.sum(grads.astype(jnp.float32), axis=0)
+    for ix in ("span", "view"):
+        bias_total = lax.psum(bias_total, axis_name=ix)
     grad_scale = 1.0 / math.sqrt(views * spans * (tok_dev // 4))
     return (merged_out[None], token_grad[None], weight_sum * grad_scale, bias_total * grad_scale)
 

time: 132 us -> 117 us (0.89)
  blocking collectives: 57.6 us -> 39.5 us
  waiting for transfers between devices: 5.71 us -> 8.72 us
    psum x1 -> x2, blocking collectives: 44 us -> 25.8 us  [body(): bias_total = lax.psum(bias_total, axis_name=ix)]
    reduce_scatter x1, waiting for transfers between devices: 0.01 us -> 3.01 us  [body(): lax.psum_scatter(partial_sum, 'view', scatter_dimension=0, tiled=True)]
  transfers between devices with their start and end apart: 4 -> 4, of which waited for: 1 -> 2; matrix products, arithmetic and copies ran while one was open for 18% -> 20% of each run, Pallas kernels for 0% -> 0%
where the time goes in v1:
time: 117 us; the launch traced here: 116 us
  blocking collectives  39.5 us (34%)
  local copies, waits for them, and re-layouts  16.6 us (14%)
  matrix products  14.4 us (12%)
  between operations  14.2 us (12%)
  starting transfers between devices  12.2 us (10%)
  other arithmetic  10.4 us (9%)
  waiting for transfers between devices  8.72 us (7%)
    psum x2, blocking collectives, body(): bias_total = lax.psum(bias_total, axis_name=ix)  25.8 us
    all_gather x1, blocking collectives, body(): all_grads = lax.all_gather(grads, 'span', axis=0, tiled=True)  13.7 us
    dot_general x1, matrix products, body(): lax.dot_general(grads, w_merge, (((1,), (1,)), ((), ())), preferred_eleme...  6.04 us
    dot_general x1, matrix products, body(): jnp.dot(merged, w_merge, preferred_element_type=jnp.float32)  5.69 us
    all_to_all x1, waiting for transfers between devices, body(): lax.all_to_all(outgoing.reshape(spans, capacity, width), 'span', split_ax...  5.69 us
    all_to_all x1, starting transfers between devices, body(): lax.all_to_all(outgoing.reshape(spans, capacity, width), 'span', split_ax...  5.19 us
    another operation x2, other arithmetic  4.84 us
    scatter x1, local copies, waits for them, and re-layouts, body(): source_of = jnp.zeros((tok_dev,), jnp.int32).at[local_index.reshape(-1)]....  4.3 us
  transfers between devices with their start and end apart: 4, of which 2 were waited for; matrix products, arithmetic and copies ran while one was open for 20% of the time, Pallas kernels for 0%

profile of v1, /device:TPU:0, one launch (start us, length us, event | category | flops | bytes accessed | tf_op | source)
XLA Modules:
  0.0 116.1 jit_solution(15012522365525005192)
XLA Ops:
  7.2 0.8 and_select_fusion.1
  8.0 4.8 %reduce-window.6 = s32[4,4,2,128]{3,2,1,0:T(2,128)S(1)} reduce-window(s32[4,4,2,128]{3,2,1,0:T(2,128)S(1)} %compare_convert_fusion, s32[]{:T(128)} %constant.19.clone.1), window={size=1x1x1x128 pad=0_0x0_0x0_0x127_0}, to_apply=%region_0.1 | reduce-window | flops 520192 | bytes 32772 | tf_op jit(solution)/shard_map/reduce-window
  13.3 0.5 broadcast.237
  13.8 1.3 %reduce.3 = s32[1024]{0:T(1024)S(1)} reduce(s32[1,1024]{1,0:T(1,128)} %param.6, s32[]{:T(128)} %broadcast.237), dimensions={0}, to_apply=%param.6.reduce_sub_computation.3 | reduce | bytes 8196 | tf_op args[1]
  15.2 2.6 %scatter_custom_fusion = bf16[384,1024]{1,0:T(8,128)(2,1)} fusion(s32[256]{0:T(256)S(1)} %bitcast.75, bf16[1,256,1024]{2,1,0:T(8,128)(2,1)S(1)} %copy-done, bf16[]{:T(256)} %constant.15.clone.1), kind=kCustom, calls=%fused_computation.13 | custom fusion | bytes 1310722 | tf_op jit(solution)/shard_map/scatter | solution.py:26
  17.8 5.2 %all-to-all-start = ((bf16[4,96,1024]{2,1,0:T(8,128)(2,1)}), bf16[4,96,1024]{2,1,0:T(8,128)(2,1)S(1)}, u32[]{:S(2)}, u32[]{:S(2)}) async-start(bf16[4,96,1024]{2,1,0:T(8,128)(2,1)} %bitcast.6), calls=%async_computation | async-start | bytes 1572864 | tf_op jit(solution)/shard_map/all_to_all | solution.py:27
  23.1 0.7 compare_select_fusion
  23.8 4.3 %scatter_custom_fusion.1 = s32[256]{0:T(256)S(1)} fusion(s32[1024]{0:T(1024)S(1)} %bitcast.78, s32[1024]{0:T(1024)S(1)} %bitcast.77, s32[]{:T(128)} %constant.19.clone.1), kind=kCustom, calls=%fused_computation.59 | custom fusion | bytes 1028 | tf_op jit(solution)/shard_map/scatter | solution.py:36
  28.2 5.7 %all-to-all-done = bf16[4,96,1024]{2,1,0:T(8,128)(2,1)S(1)} async-done(((bf16[4,96,1024]{2,1,0:T(8,128)(2,1)}), bf16[4,96,1024]{2,1,0:T(8,128)(2,1)S(1)}, u32[]{:S(2)}, u32[]{:S(2)}) %all-to-all-start) | async-done | bytes 786464 | tf_op jit(solution)/shard_map/all_to_all | solution.py:27
  33.8 1.2 %gather_fusion = bf16[256,1024]{1,0:T(8,128)(2,1)S(1)} fusion(bf16[384,1024]{1,0:T(8,128)(2,1)S(1)} %bitcast.66, s32[1024]{0:T(1024)S(1)} %pad_clamp_fusion.1), kind=kCustom, calls=%fused_computation | custom fusion | bytes 1049600 | tf_op jit(solution)/shard_map/gather | solution.py:38
  35.9 0.9 copy.20
  36.8 3.5 %all-to-all-start.2 = ((bf16[64,4,8,128]{3,2,0,1:T(8,128)(2,1)}), bf16[64,4,8,128]{3,2,0,1:T(8,128)(2,1)S(1)}, u32[]{:S(2)}, u32[]{:S(2)}) async-start(bf16[64,4,8,128]{3,2,0,1:T(8,128)(2,1)} %copy.20), calls=%async_computation.2 | async-start | bytes 1048576 | tf_op jit(solution)/shard_map/all_to_all | solution.py:65
  40.3 13.7 %all-gather = bf16[1,256,1024]{2,1,0:T(8,128)(2,1)S(1)} all-gather(bf16[1,64,1024]{2,1,0:T(8,128)(2,1)S(1)} %copy-done.1), channel_id=2, replica_groups=mesh['view'=8,'span'=4] {'span'}, dimensions={1}, use_global_device_ids=true | all-gather | bytes 655360 | tf_op jit(solution)/shard_map/all_gather | solution.py:67
  54.0 2.7 %fusion.2 = f32[1024,1024]{1,0:T(8,128)} fusion(bf16[32,8,8,128]{3,2,1,0:T(8,128)(2,1)S(1)} %bitcast.70, bf16[1,256,1024]{2,1,0:T(8,128)(2,1)S(1)} %all-gather), kind=kOutput, calls=%fused_computation.9 | convolution fusion | flops 536870912 | bytes 5242880 | tf_op jit(solution)/shard_map/dot_general | solution.py:68
  56.7 6.0 %convolution_convert_fusion = bf16[64,4096]{1,0:T(8,128)(2,1)S(1)} fusion(bf16[4096,1024]{1,0:T(8,128)(2,1)} %param.7, bf16[1,64,1024]{2,1,0:T(8,128)(2,1)S(1)} %copy-done.1), kind=kOutput, calls=%fused_computation.5 | convolution fusion | flops 537133056 | bytes 9043968 | tf_op jit(solution)/shard_map/dot_general | solution.py:48
  63.7 2.6 %scatter_custom_fusion.2 = bf16[384,1024]{1,0:T(8,128)(2,1)} fusion(s32[256]{0:T(256)S(1)} %compare_select_fusion.6, bf16[256,1024]{1,0:T(8,128)(2,1)S(1)} %reshape.267, bf16[]{:T(256)} %constant.15.clone.1), kind=kCustom, calls=%fused_computation.17 | custom fusion | bytes 786434 | tf_op jit(solution)/shard_map/scatter | solution.py:56
  66.3 3.5 %all-to-all-start.1 = ((bf16[4,96,1024]{2,1,0:T(8,128)(2,1)}), bf16[4,96,1024]{2,1,0:T(8,128)(2,1)S(1)}, u32[]{:S(2)}, u32[]{:S(2)}) async-start(bf16[4,96,1024]{2,1,0:T(8,128)(2,1)} %bitcast.14), calls=%async_computation.1 | async-start | bytes 1572864 | tf_op jit(solution)/shard_map/all_to_all | solution.py:57
  69.9 11.4 %psum.14 = f32[1024]{0:T(1024)S(1)} all-reduce(f32[1024]{0:T(1024)S(1)} %convert_reduce_fusion), channel_id=1, replica_groups=mesh['view'=8,'span'=4] {'span'}, use_global_device_ids=true, to_apply=%region_8.9 | all-reduce | flops 1024 | bytes 8192 | tf_op jit(solution)/shard_map/psum | solution.py:74
  81.2 14.5 %psum.15 = f32[1024]{0:T(1024)S(1)} all-reduce(f32[1024]{0:T(1024)S(1)} %psum.14), channel_id=1, replica_groups=mesh['view'=8,'span'=4] {'view'}, use_global_device_ids=true, to_apply=%region_9.10 | all-reduce | flops 1024 | bytes 8192 | tf_op jit(solution)/shard_map/psum | solution.py:74
  95.7 0.6 broadcast_multiply_fusion.1
  96.7 2.0 %gather_fusion.1 = bf16[256,1024]{1,0:T(8,128)(2,1)} fusion(bf16[384,1024]{1,0:T(8,128)(2,1)S(1)} %bitcast.67, s32[1024]{0:T(1024)S(1)} %pad_clamp_fusion), kind=kCustom, calls=%fused_computation.1 | custom fusion | bytes 1049600 | tf_op jit(solution)/shard_map/gather | solution.py:60
  98.7 5.7 %fusion.1 = bf16[1,64,1024]{2,1,0:T(8,128)(2,1)} fusion(bf16[64,4096]{1,0:T(8,128)(2,1)S(1)} %reshape.225, bf16[4096,1024]{1,0:T(8,128)(2,1)} %param.7, f32[1024]{0:T(1024)S(1)} %convert_element_type.18), kind=kOutput, calls=%fused_computation.8 | convolution fusion | flops 537001984 | bytes 9048064 | tf_op jit(solution)/shard_map/dot_general | solution.py:45
  104.4 3.0 %reduce-scatter.2.cloned.1.call-done = f32[128,1024]{1,0:T(8,128)} async-done(((f32[1024,1024]{1,0:T(8,128)}), f32[128,1024]{1,0:T(8,128)}) %reduce-scatter.2.cloned.1.call-update) | async-done | bytes 524304 | tf_op jit(solution)/shard_map/reduce_scatter | solution.py:71
  107.4 1.9 %broadcast_multiply_fusion = f32[128,1024]{1,0:T(8,128)} fusion(f32[128,1024]{1,0:T(8,128)} %reduce-scatter.2.cloned.1.call-done), kind=kLoop, calls=%fused_computation.21 | loop fusion | flops 131072 | bytes 1048576 | tf_op jit(solution)/shard_map/mul | solution.py:76
  (37 shorter events, 3.0 us)
Async XLA Ops:
  7.2 8.1 %copy-start = (bf16[1,256,1024]{2,1,0:T(8,128)(2,1)S(1)}, bf16[1,256,1024]{2,1,0:T(8,128)(2,1)}, u32[]{:S(2)}) copy-start(bf16[1,256,1024]{2,1,0:T(8,128)(2,1)} %param.5) | copy-start | bytes 1572868
  7.2 33.1 %copy-start.1 = (bf16[1,64,1024]{2,1,0:T(8,128)(2,1)S(1)}, bf16[1,64,1024]{2,1,0:T(8,128)(2,1)}, u32[]{:S(2)}) copy-start(bf16[1,64,1024]{2,1,0:T(8,128)(2,1)} %param.9) | copy-start | bytes 393220
  17.8 16.0 %all-to-all-start = ((bf16[4,96,1024]{2,1,0:T(8,128)(2,1)}), bf16[4,96,1024]{2,1,0:T(8,128)(2,1)S(1)}, u32[]{:S(2)}, u32[]{:S(2)}) async-start(bf16[4,96,1024]{2,1,0:T(8,128)(2,1)} %bitcast.6), calls=%async_computation | async-start | bytes 1572864 | tf_op jit(solution)/shard_map/all_to_all | solution.py:27
  36.8 17.2 %all-to-all-start.2 = ((bf16[64,4,8,128]{3,2,0,1:T(8,128)(2,1)}), bf16[64,4,8,128]{3,2,0,1:T(8,128)(2,1)S(1)}, u32[]{:S(2)}, u32[]{:S(2)}) async-start(bf16[64,4,8,128]{3,2,0,1:T(8,128)(2,1)} %copy.20), calls=%async_computation.2 | async-start | bytes 1048576 | tf_op jit(solution)/shard_map/all_to_all | solution.py:65
  40.3 67.1 %reduce-scatter.2.cloned.1.call-start = ((), (), s32[]{:S(2)}) async-start(), calls=%async_computation.4 | async-start | bytes 4718592 | tf_op jit(solution)/shard_map/reduce_scatter | solution.py:71
  56.7 13.1 %copy-start.2 = (bf16[1024]{0:T(1024)(128)(2,1)S(1)}, bf16[1024]{0:T(1024)(128)(2,1)}, u32[]{:S(2)}) copy-start(bf16[1024]{0:T(1024)(128)(2,1)} %param.8) | copy-start | bytes 6148
  66.3 30.4 %all-to-all-start.1 = ((bf16[4,96,1024]{2,1,0:T(8,128)(2,1)}), bf16[4,96,1024]{2,1,0:T(8,128)(2,1)S(1)}, u32[]{:S(2)}, u32[]{:S(2)}) async-start(bf16[4,96,1024]{2,1,0:T(8,128)(2,1)} %bitcast.14), calls=%async_computation.1 | async-start | bytes 1572864 | tf_op jit(solution)/shard_map/all_to_all | solution.py:57
Sparse Core Ops, SparseCore 0:
  56.8 50.5 reduce-scatter.1
